TPU v7x, 32 devices: a whole 2x2x4 slice. The times are simulated.
32 devices in a mesh: ctx: 8 (over y, x, core), wt: 4 (over z).
Axes of the slice: x: 2, y: 2, z: 4, core: 2. Of those that a mesh axis runs over, the one named last changes fastest.
Arguments:
- block_in: float32 [4, 1024, 896], P('wt', 'ctx'), may hold values from -6 to 6
- cotangent: float32 [4, 1024, 896], P('wt', 'ctx'), may hold values from -12 to 12
- pairs: int32 [8], replicated, may hold values from 0 to 7, as said below
- positions: int32 [4, 1024], P('wt', 'ctx'), may hold values from 0 to 1023, as said below
- params: float32 [4, 3728096], P('wt'), may hold values from -16 to 16
- moment1: float32 [4, 3728096], P('wt', 'ctx'), may hold values from -100000 to 100000
- moment2: float32 [4, 3728096], P('wt', 'ctx'), may hold values from 0 to 10000000000, as said below
Outputs:
- block_out: float32 [4, 1024, 896], P('wt', 'ctx')
- input_grad: float32 [4, 1024, 896], P('wt', 'ctx')
- param_grad: float32 [4, 3728096], P('wt', 'ctx')
- new_params: float32 [4, 3728096], P('wt', 'ctx')
- new_moment1: float32 [4, 3728096], P('wt', 'ctx')
- new_moment2: float32 [4, 3728096], P('wt', 'ctx')
Inputs may be any that keep to these rules, and one draw needn't show every extreme that they name: a permutation of 0 to 7; context index c holds blocks pairs[c] and 15 - pairs[c] of 64 tokens of every sequence. positions equals order, the causal position that pairs gives each row. `moment2`: positive.
All inputs are finite; a program needn't handle non-finite values.
Results may differ from a plain program's by a relative error of at most 0.012.
The roundings to bfloat16 on the way count: a program that leaves them out, or rounds other values in their place, can miss the bound.
Values may be sent and summed in bfloat16 or wider, within the bound.
A program may use at most 256 MiB of HBM per device.

v0:
```python
import math

import jax
import jax.numpy as jnp
from jax import lax
from jax.sharding import PartitionSpec as P

D = 896
QUERY_HEADS = 14
KEY_VALUE_HEADS = 2
HEAD_SIZE = 64
FF = 4864
QW = 896
KEY_FEATURES = 128


theta_base = 1000000.0
norm_eps = 1e-06
beta_one = 0.9
beta_two = 0.95
adam_eps = 1e-08
learn_rate = 0.02
decay_rate = 0.1
step_count = 10.0


def piece_shapes():
    return [
        (D, 0),
        (D, QW),
        (QW, 0),
        (D, KEY_FEATURES),
        (KEY_FEATURES, 0),
        (D, KEY_FEATURES),
        (KEY_FEATURES, 0),
        (QW, D),
        (D, 0),
        (FF, D),
        (FF, D),
        (FF, D),
    ]


def shard_bounds(parts):
    bounds = [0]
    for rows_full, cols in piece_shapes():
        length = rows_full // parts
        if cols > 0:
            length = length * cols
        bounds.append(bounds[-1] + length)
    return bounds


def unpack(rows_arr, parts, first, last):
    bounds = shard_bounds(parts)
    shapes = piece_shapes()
    count = rows_arr.shape[0]
    base = bounds[first]
    result = []
    for number in range(first, last):
        rows_full, cols = shapes[number]
        piece = rows_arr[:, bounds[number] - base : bounds[number + 1] - base]
        if cols > 0:
            result.append(piece.reshape(count * (rows_full // parts), cols))
        else:
            result.append(piece.reshape(-1))
    return result


def decay_mask(index_vec, parts):
    bounds = shard_bounds(parts)
    result = jnp.zeros(index_vec.shape, jnp.float32)
    for number in (1, 3, 5, 7, 9, 10, 11):
        inside = (index_vec >= bounds[number]) & (index_vec < bounds[number + 1])
        result = result + jnp.where(inside, 1.0, 0.0).astype(jnp.float32)
    return result


def rope_tables(position):
    freq_index = jnp.arange(HEAD_SIZE // 2, dtype=jnp.float32)
    inverse = jnp.exp(freq_index * (-2.0 * math.log(theta_base) / HEAD_SIZE))
    angles = position.astype(jnp.float32)[:, None] * inverse[None, :]
    cosine_table = jnp.cos(angles)
    sine_lookup = jnp.sin(angles)
    return (
        jnp.concatenate([cosine_table, cosine_table], 1),
        jnp.concatenate([sine_lookup, sine_lookup], 1),
    )


def rotary_apply(values, cosine_table, sine_lookup):
    top_half = values[..., HEAD_SIZE // 2 :]
    low_half = values[..., : HEAD_SIZE // 2]
    turned = jnp.concatenate([-top_half, low_half], -1)
    return values * cosine_table[:, None, :] + turned * sine_lookup[:, None, :]


def rotary_inverse(gradient, cosine_table, sine_lookup):
    scaled = gradient * sine_lookup[:, None, :]
    turned = jnp.concatenate([scaled[..., HEAD_SIZE // 2 :], -scaled[..., : HEAD_SIZE // 2]], -1)
    return gradient * cosine_table[:, None, :] + turned


def lookup(table, index_vec):
    slots = jnp.arange(table.shape[0], dtype=jnp.int32)
    return jnp.sum(jnp.where(index_vec[..., None] == slots, table, 0), -1)


def outer_dot(left, right):
    return lax.dot_general(
        left, right, (((0,), (0,)), ((), ())), preferred_element_type=jnp.float32
    )


def inner_dot(left, right):
    return lax.dot_general(
        left, right, (((1,), (1,)), ((), ())), preferred_element_type=jnp.float32
    )


def gate_terms(gate_pre, up_pre, d_hidden):
    sigmoid_gate = jax.nn.sigmoid(gate_pre)
    silu_gate = gate_pre * sigmoid_gate
    d_gate = (d_hidden * up_pre * sigmoid_gate * (1.0 + gate_pre * (1.0 - sigmoid_gate))).astype(
        jnp.bfloat16
    )
    d_up = (d_hidden * silu_gate).astype(jnp.bfloat16)
    return (d_gate, d_up)


def hidden_units(gate_pre, up_pre):
    return (gate_pre * jax.nn.sigmoid(gate_pre) * up_pre).astype(jnp.bfloat16)


def body(block_in, cotangent, pairs, positions, params, moment1, moment2):
    n_ctx = lax.axis_size("ctx")
    n_wt = lax.axis_size("wt")
    token_rows = block_in.shape[1]
    half_rows = token_rows // 2
    seq_len = token_rows * n_ctx
    key_tile = min(512, seq_len)
    query_group_width = QUERY_HEADS // KEY_VALUE_HEADS
    score_scale = 1.0 / math.sqrt(HEAD_SIZE)
    ctx_id = lax.axis_index("ctx")
    wt_id = lax.axis_index("wt")
    x_rows = block_in[0]
    cot_rows = cotangent[0]
    row_bf = params.astype(jnp.bfloat16)
    prefix = shard_bounds(n_wt)[9]
    attn_all = lax.all_gather(row_bf[:, :prefix], "wt", axis=0, tiled=True)
    gain_b, wq_b, bq_b, wk_b, bk_b, wv_b, bv_b, wo_b, gain_two = unpack(attn_all, n_wt, 0, 9)
    gain_full = gain_b.astype(jnp.float32)
    inv_rms = lax.rsqrt(jnp.mean(x_rows * x_rows, -1, keepdims=True) + norm_eps)
    normed = (x_rows * inv_rms * gain_full).astype(jnp.bfloat16)
    queries = jnp.dot(normed, wq_b, preferred_element_type=jnp.float32) + bq_b.astype(jnp.float32)
    key_projected = jnp.dot(normed, wk_b, preferred_element_type=jnp.float32) + bk_b.astype(
        jnp.float32
    )
    value_projected = jnp.dot(normed, wv_b, preferred_element_type=jnp.float32) + bv_b.astype(
        jnp.float32
    )
    cosine_table, sine_lookup = rope_tables(positions[0])
    query_narrow = rotary_apply(
        queries.reshape(token_rows, QUERY_HEADS, HEAD_SIZE), cosine_table, sine_lookup
    ).astype(jnp.bfloat16)
    key_narrow = rotary_apply(
        key_projected.reshape(token_rows, KEY_VALUE_HEADS, HEAD_SIZE), cosine_table, sine_lookup
    ).astype(jnp.bfloat16)
    value_narrow = value_projected.astype(jnp.bfloat16)
    own_kv = jnp.concatenate([key_narrow.reshape(token_rows, KEY_FEATURES), value_narrow], 1)
    all_kv = lax.all_gather(own_kv, "ctx", axis=0, tiled=True)
    block_ids = jnp.arange(2 * n_ctx, dtype=jnp.int32)
    target = jnp.where(block_ids < n_ctx, block_ids, 2 * n_ctx - 1 - block_ids)
    owner = jnp.sum(
        jnp.where(
            pairs[None, :] == target[:, None], jnp.arange(n_ctx, dtype=jnp.int32)[None, :], 0
        ),
        1,
    )
    late_side = (block_ids >= n_ctx).astype(jnp.int32)
    causal_ids = jnp.arange(seq_len, dtype=jnp.int32)
    block_of = causal_ids // half_rows
    source_row = (
        lookup(owner, block_of) * token_rows
        + lookup(late_side, block_of) * half_rows
        + causal_ids % half_rows
    )
    sorted_kv = jnp.take(all_kv, source_row, axis=0)
    early_block = lookup(pairs, ctx_id)
    late_block = 2 * n_ctx - 1 - early_block

    def query_positions(block_now):
        return block_now * half_rows + jnp.arange(half_rows, dtype=jnp.int32)

    def tile_total(block_now):
        return ((block_now + 1) * half_rows + key_tile - 1) // key_tile

    def key_slice(tile_no):
        tile_start = tile_no * key_tile
        key_value_tile = lax.dynamic_slice_in_dim(sorted_kv, tile_start, key_tile, 0)
        key_block_tile = key_value_tile[:, :KEY_FEATURES].reshape(
            key_tile, KEY_VALUE_HEADS, HEAD_SIZE
        )
        value_tile = key_value_tile[:, KEY_FEATURES:].reshape(key_tile, KEY_VALUE_HEADS, HEAD_SIZE)
        k_pos = tile_start + jnp.arange(key_tile, dtype=jnp.int32)
        return (tile_start, key_block_tile, value_tile, k_pos)

    def attend(query_half, block_now):
        q_pos = query_positions(block_now)
        query_group = query_half.reshape(half_rows, KEY_VALUE_HEADS, query_group_width, HEAD_SIZE)

        def tile_scores(tile_no):
            tile_start, key_block_tile, value_tile, k_pos = key_slice(tile_no)
            scores = score_scale * jnp.einsum(
                "qkgd,tkd->kgqt", query_group, key_block_tile, preferred_element_type=jnp.float32
            )
            visible = k_pos[None, :] <= q_pos[:, None]
            return (jnp.where(visible, scores, -jnp.inf), value_tile)

        def total_step(tile_no, state_carry):
            run_peak, run_total = state_carry
            scores, value_tile = tile_scores(tile_no)
            new_peak = jnp.maximum(run_peak, jnp.max(scores, -1))
            factor = jnp.exp(run_peak - new_peak)
            run_total = run_total * factor + jnp.sum(jnp.exp(scores - new_peak[..., None]), -1)
            return (new_peak, run_total)

        tile_count = tile_total(block_now)
        initial_state = (
            jnp.full((KEY_VALUE_HEADS, query_group_width, half_rows), -jnp.inf, jnp.float32),
            jnp.zeros((KEY_VALUE_HEADS, query_group_width, half_rows), jnp.float32),
        )
        run_peak, run_total = lax.fori_loop(0, tile_count, total_step, initial_state)
        log_total = run_peak + jnp.log(run_total)

        def value_step(tile_no, run_accum):
            scores, value_tile = tile_scores(tile_no)
            prob_bf = jnp.exp(scores - log_total[..., None]).astype(jnp.bfloat16)
            return run_accum + jnp.einsum(
                "kgqt,tkd->kgqd", prob_bf, value_tile, preferred_element_type=jnp.float32
            )

        run_accum = lax.fori_loop(
            0,
            tile_count,
            value_step,
            jnp.zeros((KEY_VALUE_HEADS, query_group_width, half_rows, HEAD_SIZE), jnp.float32),
        )
        context_half = jnp.transpose(run_accum, (2, 0, 1, 3)).reshape(half_rows, QW)
        return (context_half, log_total)

    query_flat = query_narrow.reshape(token_rows, QW)
    ctx_early, lse_early = attend(query_flat[:half_rows], early_block)
    ctx_late, lse_late = attend(query_flat[half_rows:], late_block)
    context_rows = jnp.concatenate([ctx_early, ctx_late], 0)
    context_bf = context_rows.astype(jnp.bfloat16)
    feature_cols, context_cols = (
        lax.all_to_all(normed, "wt", split_axis=1, concat_axis=0, tiled=True),
        lax.all_to_all(context_bf, "wt", split_axis=1, concat_axis=0, tiled=True),
    )
    mid_rows = x_rows + jnp.dot(context_bf, wo_b, preferred_element_type=jnp.float32)
    gain_two_full = gain_two.astype(jnp.float32)
    inv_rms_two = lax.rsqrt(jnp.mean(mid_rows * mid_rows, -1, keepdims=True) + norm_eps)
    normed_two = (mid_rows * inv_rms_two * gain_two_full).astype(jnp.bfloat16)
    cot_bf = cot_rows.astype(jnp.bfloat16)
    normed_group, cot_group = (
        lax.all_gather(normed_two, "wt", axis=0, tiled=True),
        lax.all_gather(cot_bf, "wt", axis=0, tiled=True),
    )
    wg_own, wu_own, wd_own = unpack(row_bf[:, prefix:], n_wt, 9, 12)
    gate_pre = inner_dot(normed_group, wg_own)
    up_pre = inner_dot(normed_group, wu_own)
    hidden_bf = hidden_units(gate_pre, up_pre)
    ff_sum = lax.psum_scatter(
        jnp.dot(hidden_bf, wd_own, preferred_element_type=jnp.float32),
        "wt",
        scatter_dimension=0,
        tiled=True,
    )
    d_hidden = inner_dot(cot_group, wd_own)
    d_gate, d_up = gate_terms(gate_pre, up_pre, d_hidden)
    grad_wg = outer_dot(d_gate, normed_group)
    grad_wu = outer_dot(d_up, normed_group)
    grad_wd = outer_dot(hidden_bf, cot_group)
    d_norm_two = lax.psum_scatter(
        jnp.dot(d_gate, wg_own, preferred_element_type=jnp.float32)
        + jnp.dot(d_up, wu_own, preferred_element_type=jnp.float32),
        "wt",
        scatter_dimension=0,
        tiled=True,
    )
    block_out = mid_rows + ff_sum
    grad_gain_two = jnp.sum(d_norm_two * mid_rows * inv_rms_two, 0)
    d_scaled_two = d_norm_two * gain_two_full
    d_mid = (
        cot_rows
        + inv_rms_two * d_scaled_two
        - mid_rows
        * (inv_rms_two * inv_rms_two * inv_rms_two)
        * jnp.mean(d_scaled_two * mid_rows, -1, keepdims=True)
    )
    d_mid_bf = d_mid.astype(jnp.bfloat16)
    context_gradient = inner_dot(d_mid_bf, wo_b)
    context_gradient_narrow = context_gradient.astype(jnp.bfloat16)
    delta_rows = jnp.sum(
        (context_gradient * context_rows).reshape(
            token_rows, KEY_VALUE_HEADS, query_group_width, HEAD_SIZE
        ),
        -1,
    )

    def attend_back(query_half, half_gradient, lse_half, delta_half, block_now, key_gradients):
        q_pos = query_positions(block_now)
        query_group = query_half.reshape(half_rows, KEY_VALUE_HEADS, query_group_width, HEAD_SIZE)
        group_gradient = half_gradient.reshape(
            half_rows, KEY_VALUE_HEADS, query_group_width, HEAD_SIZE
        )
        delta_t = jnp.transpose(delta_half, (1, 2, 0))[..., None]

        def tile_step(tile_no, state_carry):
            d_query, key_gradients = state_carry
            tile_start, key_block_tile, value_tile, k_pos = key_slice(tile_no)
            scores = score_scale * jnp.einsum(
                "qkgd,tkd->kgqt", query_group, key_block_tile, preferred_element_type=jnp.float32
            )
            visible = k_pos[None, :] <= q_pos[:, None]
            scores = jnp.where(visible, scores, -jnp.inf)
            prob_tile = jnp.where(visible, jnp.exp(scores - lse_half[..., None]), 0.0)
            prob_bf = prob_tile.astype(jnp.bfloat16)
            d_probs = jnp.einsum(
                "qkgd,tkd->kgqt", group_gradient, value_tile, preferred_element_type=jnp.float32
            )
            d_scores = (prob_tile * (d_probs - delta_t)).astype(jnp.bfloat16)
            d_query = d_query + score_scale * jnp.einsum(
                "kgqt,tkd->qkgd", d_scores, key_block_tile, preferred_element_type=jnp.float32
            )
            key_part = score_scale * jnp.einsum(
                "kgqt,qkgd->tkd", d_scores, query_group, preferred_element_type=jnp.float32
            )
            value_part = jnp.einsum(
                "kgqt,qkgd->tkd", prob_bf, group_gradient, preferred_element_type=jnp.float32
            )
            update = jnp.concatenate(
                [
                    key_part.reshape(key_tile, KEY_FEATURES),
                    value_part.reshape(key_tile, KEY_FEATURES),
                ],
                1,
            )
            current = lax.dynamic_slice_in_dim(key_gradients, tile_start, key_tile, 0)
            key_gradients = lax.dynamic_update_slice_in_dim(
                key_gradients, current + update, tile_start, 0
            )
            return (d_query, key_gradients)

        initial_state = (
            jnp.zeros((half_rows, KEY_VALUE_HEADS, query_group_width, HEAD_SIZE), jnp.float32),
            key_gradients,
        )
        return lax.fori_loop(0, tile_total(block_now), tile_step, initial_state)

    key_gradients = jnp.zeros((seq_len, 2 * KEY_FEATURES), jnp.float32)
    dq_early, key_gradients = attend_back(
        query_flat[:half_rows],
        context_gradient_narrow[:half_rows],
        lse_early,
        delta_rows[:half_rows],
        early_block,
        key_gradients,
    )
    dq_late, key_gradients = attend_back(
        query_flat[half_rows:],
        context_gradient_narrow[half_rows:],
        lse_late,
        delta_rows[half_rows:],
        late_block,
        key_gradients,
    )
    d_query_rot = jnp.concatenate([dq_early, dq_late], 0).reshape(
        token_rows, QUERY_HEADS, HEAD_SIZE
    )
    d_query = rotary_inverse(d_query_rot, cosine_table, sine_lookup).reshape(token_rows, QW)
    row_ids = jnp.arange(seq_len, dtype=jnp.int32)
    local_ids = row_ids % token_rows
    chosen = lookup(pairs, row_ids // token_rows)
    back_block = jnp.where(local_ids < half_rows, chosen, 2 * n_ctx - 1 - chosen)
    back_index = back_block * half_rows + local_ids % half_rows
    per_device = jnp.take(key_gradients, back_index, axis=0)
    owned_gradients = lax.psum_scatter(per_device, "ctx", scatter_dimension=0, tiled=True)
    key_gradient = rotary_inverse(
        owned_gradients[:, :KEY_FEATURES].reshape(token_rows, KEY_VALUE_HEADS, HEAD_SIZE),
        cosine_table,
        sine_lookup,
    ).reshape(token_rows, KEY_FEATURES)
    value_gradient = owned_gradients[:, KEY_FEATURES:]
    dq_bf = d_query.astype(jnp.bfloat16)
    dk_bf = key_gradient.astype(jnp.bfloat16)
    dv_bf = value_gradient.astype(jnp.bfloat16)
    d_norm = inner_dot(dq_bf, wq_b) + inner_dot(dk_bf, wk_b) + inner_dot(dv_bf, wv_b)
    grad_gain = jnp.sum(d_norm * x_rows * inv_rms, 0)
    d_scaled = d_norm * gain_full
    d_input = inv_rms * d_scaled - x_rows * (inv_rms * inv_rms * inv_rms) * jnp.mean(
        d_scaled * x_rows, -1, keepdims=True
    )
    input_grad = d_mid + d_input
    mid_group, query_grads, key_grads_group, value_grads_group = (
        lax.all_gather(d_mid_bf, "wt", axis=0, tiled=True),
        lax.all_gather(dq_bf, "wt", axis=0, tiled=True),
        lax.all_gather(dk_bf, "wt", axis=0, tiled=True),
        lax.all_gather(dv_bf, "wt", axis=0, tiled=True),
    )
    gain_part, gain_two_part = (
        lax.psum_scatter(grad_gain, "wt", scatter_dimension=0, tiled=True),
        lax.psum_scatter(grad_gain_two, "wt", scatter_dimension=0, tiled=True),
    )
    grad_wq = outer_dot(feature_cols, query_grads)
    grad_wk = outer_dot(feature_cols, key_grads_group)
    grad_wv = outer_dot(feature_cols, value_grads_group)
    grad_wo = outer_dot(context_cols, mid_group)
    query_part = QW // n_wt
    key_part_len = KEY_FEATURES // n_wt
    bias_q = lax.dynamic_slice_in_dim(
        jnp.sum(query_grads.astype(jnp.float32), 0), wt_id * query_part, query_part, 0
    )
    bias_k = lax.dynamic_slice_in_dim(
        jnp.sum(key_grads_group.astype(jnp.float32), 0), wt_id * key_part_len, key_part_len, 0
    )
    bias_v = lax.dynamic_slice_in_dim(
        jnp.sum(value_grads_group.astype(jnp.float32), 0), wt_id * key_part_len, key_part_len, 0
    )
    shard_grad = jnp.concatenate(
        [
            gain_part,
            grad_wq.reshape(-1),
            bias_q,
            grad_wk.reshape(-1),
            bias_k,
            grad_wv.reshape(-1),
            bias_v,
            grad_wo.reshape(-1),
            gain_two_part,
            grad_wg.reshape(-1),
            grad_wu.reshape(-1),
            grad_wd.reshape(-1),
        ]
    )
    grad_piece = lax.psum_scatter(shard_grad, "ctx", scatter_dimension=0, tiled=True)
    piece_len = moment1.shape[1]
    param_grad = grad_piece.reshape(1, piece_len)
    piece_start = ctx_id * piece_len
    own_params = lax.dynamic_slice_in_dim(params[0], piece_start, piece_len, 0).reshape(
        1, piece_len
    )
    decay = decay_mask(piece_start + jnp.arange(piece_len, dtype=jnp.int32), n_wt).reshape(
        1, piece_len
    )
    new_moment1 = beta_one * moment1 + (1.0 - beta_one) * param_grad
    new_moment2 = beta_two * moment2 + (1.0 - beta_two) * param_grad * param_grad
    m_hat = new_moment1 / (1.0 - beta_one**step_count)
    v_hat = new_moment2 / (1.0 - beta_two**step_count)
    new_params = own_params - learn_rate * (
        m_hat / (jnp.sqrt(v_hat) + adam_eps) + decay_rate * decay * own_params
    )
    return (
        block_out.reshape(1, token_rows, D),
        input_grad.reshape(1, token_rows, D),
        param_grad,
        new_params,
        new_moment1,
        new_moment2,
    )


def solution(mesh):
    in_specs = (
        P("wt", "ctx", None),
        P("wt", "ctx", None),
        P(),
        P("wt", "ctx"),
        P("wt", None),
        P("wt", "ctx"),
        P("wt", "ctx"),
    )
    out_specs = (
        P("wt", "ctx", None),
        P("wt", "ctx", None),
        P("wt", "ctx"),
        P("wt", "ctx"),
        P("wt", "ctx"),
        P("wt", "ctx"),
    )
    return jax.shard_map(body, mesh=mesh, in_specs=in_specs, out_specs=out_specs, check_vma=False)
```

profile of v0, /device:TPU:0, one launch (start us, length us, event | category | flops | bytes accessed | tf_op | source)
XLA Modules:
  0.0 831.1 jit_solution(18370185866348542281)
XLA Ops:
  7.2 12.8 %convert_element_type.161 = bf16[1,3728096]{1,0:T(2,128)(2,1)S(1)} convert(f32[1,3728096]{1,0:T(1,128)} %param.23) | non-fusion elementwise | flops 3728096 | bytes 22368576 | tf_op jit(solution)/shard_map/convert_element_type | solution.py:148
  20.0 5.3 copy-done
  25.3 3.0 slice_bitcast_fusion
  31.6 50.3 %slice_reduce_fusion = (bf16[1089536]{0:T(1024)(128)(2,1)S(1)}, bf16[1089536]{0:T(1024)(128)(2,1)}, bf16[1089536]{0:T(1024)(128)(2,1)}) fusion(bf16[1,3728096]{1,0:T(2,128)(2,1)} %copy-done), kind=kLoop, calls=%fused_computation.105 | loop fusion | bytes 13074432 | tf_op jit(solution)/shard_map/slice | solution.py:62
  81.9 5.0 reshape.683
  86.9 5.0 reshape.684
  91.9 3.3 reshape.685
  95.9 36.5 %all_gather.27 = bf16[512,896]{1,0:T(8,128)(2,1)} all-gather(bf16[128,896]{1,0:T(8,128)(2,1)S(1)} %bitcast_convert_fusion), channel_id=1, replica_groups=mesh['ctx'=8,'wt'=4] {'wt'}, dimensions={0}, use_global_device_ids=true | all-gather | bytes 1146880 | tf_op jit(solution)/shard_map/all_gather | solution.py:268
  132.4 46.1 %all-gather.3.cloned.1.call-done = bf16[4,1,459488]{2,1,0:T(2,128)(2,1)} async-done(((bf16[1,1,459488]{2,1,0:T(2,128)(2,1)}), bf16[4,1,459488]{2,1,0:T(2,128)(2,1)}) %all-gather.3.cloned.1.call-update) | async-done | bytes 3675920 | tf_op jit(solution)/shard_map/all_gather | solution.py:150
  178.5 6.7 copy.197
  185.2 2.3 fusion.123
  187.9 2.2 reshape.682
  191.7 9.9 %all_gather.25 = bf16[1024,256]{0,1:T(8,128)(2,1)S(1)} all-gather(bf16[128,256]{0,1:T(8,128)(2,1)S(1)} %pad_maximum_fusion.3), channel_id=1, replica_groups=mesh['ctx'=8,'wt'=4] {'ctx'}, dimensions={0}, use_global_device_ids=true | all-gather | bytes 589824 | tf_op jit(solution)/shard_map/all_gather | solution.py:171
  201.8 3.9 gather_fusion
  206.2 2.5 reshape.676
  208.8 1.2 convolution_add_fusion.4
  210.0 1.2 copy.133
  215.8 2.4 while.76
  218.3 2.1 while.77
  221.5 1.9 reshape.681
  223.5 1.6 constant_dynamic-update-slice_fusion
  225.1 1.7 multiply_reduce_fusion.2
  226.9 19.8 %all_gather.26 = bf16[512,896]{1,0:T(8,128)(2,1)S(1)} all-gather(bf16[128,896]{1,0:T(8,128)(2,1)S(1)} %multiply_convert_fusion.4), channel_id=1, replica_groups=mesh['ctx'=8,'wt'=4] {'wt'}, dimensions={0}, use_global_device_ids=true | all-gather | bytes 1146880 | tf_op jit(solution)/shard_map/all_gather | solution.py:267
  246.8 1.5 fusion.131
  248.7 1.5 fusion.132
  250.6 3.6 multiply_convert_fusion
  254.2 1.5 fusion.134
  255.8 2.8 convolution_add_fusion
  258.6 4.8 fusion.133
  265.8 1.9 multiply_convert_fusion.3
  267.7 4.0 all-to-all-start
  273.9 1.2 concatenate.60
  277.1 1.9 concatenate.59
  278.9 1.8 pad_maximum_fusion.2
  280.7 1.8 copy.155
  282.6 5.0 fusion.136
  287.6 5.2 reshape.698
  292.7 5.0 fusion.137
  297.7 5.1 reshape.699
  302.8 5.0 fusion.138
  307.8 5.3 reshape.700
  314.3 27.6 %reduce-scatter.4.cloned.1.call-done = f32[128,896]{1,0:T(8,128)} async-done(((f32[512,896]{1,0:T(8,128)}), f32[128,896]{1,0:T(8,128)}) %reduce-scatter.4.cloned.1.call-update) | async-done | bytes 458768 | tf_op jit(solution)/shard_map/reduce_scatter | solution.py:274
  341.8 2.5 fusion.119
  346.2 3.6 while.78
  346.4 1.6 fusion.280
  350.1 5.2 while.79
  356.6 3.5 gather_fusion.1
  362.3 19.3 %all_gather.28 = bf16[512,896]{0,1:T(8,128)(2,1)S(1)} all-gather(bf16[128,896]{0,1:T(8,128)(2,1)S(1)} %fusion.71), channel_id=1, replica_groups=mesh['ctx'=8,'wt'=4] {'wt'}, dimensions={0}, use_global_device_ids=true | all-gather | bytes 1146880 | tf_op jit(solution)/shard_map/all_gather | solution.py:408
  381.6 3.4 all-to-all-start.1
  385.1 1.5 fusion.89
  387.5 21.9 %all_gather.31 = bf16[512,896]{1,0:T(8,128)(2,1)} all-gather(bf16[128,896]{1,0:T(8,128)(2,1)S(1)} %copy-done.20), channel_id=1, replica_groups=mesh['ctx'=8,'wt'=4] {'wt'}, dimensions={0}, use_global_device_ids=true | all-gather | bytes 1146880 | tf_op jit(solution)/shard_map/all_gather | solution.py:407
  409.4 2.6 fusion.84
  412.0 2.1 reshape.697
  414.4 2.3 fusion.135
  418.5 12.3 %all_gather.29 = bf16[512,128]{0,1:T(8,128)(2,1)S(1)} all-gather(bf16[128,128]{0,1:T(8,128)(2,1)S(1)} %fusion.98), channel_id=1, replica_groups=mesh['ctx'=8,'wt'=4] {'wt'}, dimensions={0}, use_global_device_ids=true | all-gather | bytes 163840 | tf_op jit(solution)/shard_map/all_gather | solution.py:409
  430.8 1.3 convolution_add_fusion.2
  432.2 12.4 %all_gather.30 = bf16[512,128]{0,1:T(8,128)(2,1)S(1)} all-gather(bf16[128,128]{0,1:T(8,128)(2,1)S(1)} %slice.215), channel_id=1, replica_groups=mesh['ctx'=8,'wt'=4] {'wt'}, dimensions={0}, use_global_device_ids=true | all-gather | bytes 163840 | tf_op jit(solution)/shard_map/all_gather | solution.py:410
  445.9 8.5 %all-reduce.3 = (f32[896]{0:T(1024)S(1)}, f32[896]{0:T(1024)S(1)}) all-reduce(f32[896]{0:T(1024)S(1)} %get-tuple-element.643, f32[896]{0:T(1024)S(1)} %get-tuple-element.641), channel_id=5, replica_groups=mesh['ctx'=8,'wt'=4] {'wt'}, use_global_device_ids=true, to_apply=%region_30.31.clone | all-reduce | flops 1792 | bytes 14336
  456.9 125.2 %concatenate.62 = f32[3728096]{0:T(1024)} concatenate(f32[224]{0:T(256)S(1)} %dynamic-slice.2, f32[200704]{0:T(1024)S(1)} %copy-done.14, f32[224]{0:T(256)S(1)} %dynamic_slice.36, f32[28672]{0:T(1024)S(1)} %convolution_bitcast_fusion.3, f32[32]{0:T(128)S(1)} %dynamic_slice.37, f32[28672]{0:T(1024)S(1)} %convolution_bitcast_fusion.2, f32[32]{0:T(128)S(1)} %dynamic_slice.38, ...), dimensions={0} | concatenate | bytes 29824768 | tf_op jit(solution)/shard_map/concatenate | solution.py:431
  585.0 194.6 %all-reduce.6.cloned.1.call-done = f32[3728096]{0:T(1024)} async-done(((f32[3728096]{0:T(1024)}), f32[3728096]{0:T(1024)}) %all-reduce.6.cloned.1.call-update) | async-done | bytes 14912400
  779.5 2.1 broadcast_multiply_fusion
  781.6 9.5 %reshape.701 = f32[1,466012]{1,0:T(1,128)} reshape(f32[466012]{0:T(1024)S(1)} %get-tuple-element.749) | data formatting | bytes 3728096 | tf_op jit(solution)/shard_map/reshape | solution.py:449
  791.3 1.3 copy-done.25
  793.2 31.0 %multiply_subtract_fusion = (f32[1,466012]{1,0:T(1,128)}, f32[1,466012]{1,0:T(1,128)}, f32[1,466012]{1,0:T(1,128)}) fusion(f32[1,3728096]{1,0:T(1,128)} %param.23, s32[]{:T(128)S(6)} %select_n.312, s32[]{:T(128)S(6)} %mul.585, f32[466012]{0:T(1024)S(1)} %get-tuple-element.748, f32[1,466012]{1,0:T(1,128)S(1)} %copy-done.25, ...), kind=kLoop, calls=%fused_computation.124 | loop fusion | flops 22368576 | bytes 14912392 | tf_op jit(solution)/shard_map/sub | solution.py:461
  (267 shorter events, 46.0 us)
Async XLA Ops:
  7.2 171.3 %all-gather.3.cloned.1.call-start = ((), (), s32[]{:S(2)}) async-start(), calls=%async_computation.8 | async-start | bytes 9190400 | tf_op jit(solution)/shard_map/all_gather | solution.py:150
  20.0 5.3 copy-start
  25.3 3.1 copy-start.33
  28.3 284.8 %reduce-scatter.6.cloned.1.call-start = ((), (), s32[]{:S(2)}) async-start(), calls=%async_computation.6 | async-start | bytes 2293760 | tf_op jit(solution)/shard_map/reduce_scatter | solution.py:285
  91.9 3.4 copy-start.34
  91.9 3.7 copy-start.1
  91.9 3.9 copy-start.27
  190.5 1.2 copy-start.23
  190.8 11.0 %copy-start.21 = (bf16[896,128]{1,0:T(8,128)(2,1)}, bf16[896,128]{1,0:T(8,128)(2,1)S(1)}, u32[]{:S(2)}) copy-start(bf16[896,128]{1,0:T(8,128)(2,1)S(1)} %reshape.673) | copy-start | bytes 688132
  208.7 2.6 copy-start.2
  211.5 0.7 copy-start.5
  214.4 1.3 copy-start.11
  220.4 3.0 copy-start.12
  220.4 4.7 copy-start.4
  225.1 21.7 %copy-start.8 = (bf16[1216,896]{1,0:T(8,128)(2,1)S(1)}, bf16[1216,896]{1,0:T(8,128)(2,1)}, u32[]{:S(2)}) copy-start(bf16[1216,896]{1,0:T(8,128)(2,1)} %reshape.683) | copy-start | bytes 6537220
  246.8 1.5 copy-start.9
  246.8 1.9 copy-start.18
  248.7 1.6 copy-start.7
  248.7 1.8 copy-start.13
  254.2 1.5 copy-start.10
  254.2 1.6 copy-start.17
  258.6 83.3 %reduce-scatter.4.cloned.1.call-start = ((), (), s32[]{:S(2)}) async-start(), calls=%async_computation.5 | async-start | bytes 2293760 | tf_op jit(solution)/shard_map/reduce_scatter | solution.py:274
  263.4 1.0 copy-start.36
  267.7 113.9 %all-to-all-start = ((bf16[128,4,224]{0,2,1:T(8,128)(2,1)}), bf16[128,4,224]{0,2,1:T(8,128)(2,1)}, u32[]{:S(2)}, u32[]{:S(2)}) async-start(bf16[128,4,224]{0,2,1:T(8,128)(2,1)} %multiply_convert_fusion.3), calls=%async_computation.3 | async-start | bytes 458752 | tf_op jit(solution)/shard_map/all_to_all | solution.py:258
  271.7 144.9 %reduce-scatter.8.cloned.1.call-start = ((), (), s32[]{:S(2)}) async-start(), calls=%async_computation.7 | async-start | bytes 1179648 | tf_op jit(solution)/shard_map/reduce_scatter | solution.py:389
  341.8 2.5 copy-start.16
  344.3 1.3 copy-start.19
  346.2 3.6 copy-start.31
  348.5 0.9 copy-start.6
  360.4 1.1 copy-start.30
  381.6 27.8 %all-to-all-start.1 = ((bf16[128,4,224]{0,2,1:T(8,128)(2,1)}), bf16[128,4,224]{0,2,1:T(8,128)(2,1)S(1)}, u32[]{:S(2)}, u32[]{:S(2)}) async-start(bf16[128,4,224]{0,2,1:T(8,128)(2,1)} %copy.155), calls=%async_computation.4 | async-start | bytes 458752 | tf_op jit(solution)/shard_map/all_to_all | solution.py:259
  385.0 2.5 copy-start.20
  385.0 394.5 %all-reduce.6.cloned.1.call-start = ((), (), s32[]{:S(2)}) async-start(), calls=%async_computation.9 | async-start | bytes 29827072
  409.4 5.0 copy-start.3
  414.1 16.7 %copy-start.22 = (bf16[896,128]{1,0:T(8,128)(2,1)S(1)}, bf16[896,128]{1,0:T(8,128)(2,1)}, u32[]{:S(2)}) copy-start(bf16[896,128]{1,0:T(8,128)(2,1)} %copy-done.21) | copy-start | bytes 688132
  416.7 28.2 %copy-start.24 = (bf16[896,128]{1,0:T(8,128)(2,1)S(1)}, bf16[896,128]{1,0:T(8,128)(2,1)}, u32[]{:S(2)}) copy-start(bf16[896,128]{1,0:T(8,128)(2,1)} %copy-done.23) | copy-start | bytes 688132
  416.7 15.5 %copy-start.32 = (f32[128,256]{0,1:T(8,128)S(1)}, f32[128,256]{0,1:T(8,128)}, u32[]{:S(2)}) copy-start(f32[128,256]{0,1:T(8,128)} %reduce-scatter.8.cloned.1.call-done) | copy-start | bytes 393220
  432.0 24.9 %copy-start.14 = (f32[200704]{0:T(1024)S(1)}, f32[200704]{0:T(1024)}, u32[]{:S(2)}) copy-start(f32[200704]{0:T(1024)} %reshape.694) | copy-start | bytes 2408452
  432.0 24.9 %copy-start.15 = (f32[200704]{0:T(1024)S(1)}, f32[200704]{0:T(1024)}, u32[]{:S(2)}) copy-start(f32[200704]{0:T(1024)} %reshape.697) | copy-start | bytes 2408452
  582.1 0.7 copy-start.35
  582.1 1.9 copy-start.28
  582.1 1.9 copy-start.29
  791.1 1.5 copy-start.25
  791.1 2.1 copy-start.26
Sparse Core Ops, SparseCore 0:
  28.4 150.0 all-gather.2
  258.7 41.3 reduce-scatter.5
  302.9 38.8 reduce-scatter.3
  361.6 34.9 reduce-scatter.7
  582.3 197.2 all-reduce.5
where the time goes:
time: 848 us; the launch traced here: 831 us
  local copies, waits for them, and re-layouts  272 us (32%)
  waiting for transfers between devices  268 us (32%)
  blocking collectives  141 us (17%)
  other arithmetic  65.5 us (8%)
  matrix products  57.2 us (7%)
  between operations  19.1 us (2%)
    unnamed x6, waiting for transfers between devices  195 us
    concatenate x1, local copies, waits for them, and re-layouts, body(): jnp.concatenate([gain_part, grad_wq.reshape(-1), bias_q, grad_wk.reshape(...  125 us
    slice x3, local copies, waits for them, and re-layouts, unpack(): piece = rows_arr[:, bounds[number] - base:bounds[number + 1] - base]  52.9 us
    all_gather x1, waiting for transfers between devices, body(): attn_all = lax.all_gather(row_bf[:, :prefix], 'wt', axis=0, tiled=True)  46.1 us
    all_gather x1, blocking collectives, body(): lax.all_gather(cot_bf, 'wt', axis=0, tiled=True)  36.5 us
    sub x1, other arithmetic, body(): own_params - learn_rate * (m_hat / (jnp.sqrt(v_hat) + adam_eps) + decay_r...  31 us
    reduce_scatter x1, waiting for transfers between devices, body(): lax.psum_scatter(jnp.dot(hidden_bf, wd_own, preferred_element_type=jnp.fl...  27.6 us
    unnamed x85, local copies, waits for them, and re-layouts  22.7 us
  transfers between devices with their start and end apart: 7, of which 3 were waited for; matrix products, arithmetic and copies ran while one was open for 18% of the time, Pallas kernels for 0%

commit v1 on v0

--- a/solution.py
+++ b/solution.py
@@ -147,8 +147,27 @@
     cot_rows = cotangent[0]
     row_bf = params.astype(jnp.bfloat16)
     prefix = shard_bounds(n_wt)[9]
-    attn_all = lax.all_gather(row_bf[:, :prefix], "wt", axis=0, tiled=True)
-    gain_b, wq_b, bq_b, wk_b, bk_b, wv_b, bv_b, wo_b, gain_two = unpack(attn_all, n_wt, 0, 9)
+    g1_s, wq_s, bq_s, wk_s, bk_s, wv_s, bv_s, wo_s, g2_s = unpack(row_bf[:, :prefix], n_wt, 0, 9)
+    shard_rows = D // n_wt
+    wide = 2 * QW + 2 * KEY_FEATURES
+    vec = jnp.concatenate([g1_s, bq_s, bk_s, bv_s, g2_s])
+    vec_rows = jnp.pad(vec.reshape(1, -1), ((0, 15), (0, wide - vec.shape[0])))
+    attn_own = jnp.concatenate(
+        [jnp.concatenate([wq_s, wo_s, wk_s, wv_s], 1), vec_rows], 0
+    )
+    attn_all = lax.all_gather(attn_own, "wt", axis=0, tiled=False)
+    mats = attn_all[:, :shard_rows].reshape(D, wide)
+    wq_b = mats[:, :QW]
+    wo_b = mats[:, QW : 2 * QW]
+    wk_b = mats[:, 2 * QW : 2 * QW + KEY_FEATURES]
+    wv_b = mats[:, 2 * QW + KEY_FEATURES :]
+    vecs = attn_all[:, shard_rows]
+    vec_parts = []
+    vec_at = 0
+    for own in (g1_s, bq_s, bk_s, bv_s, g2_s):
+        vec_parts.append(vecs[:, vec_at : vec_at + own.shape[0]].reshape(-1))
+        vec_at += own.shape[0]
+    gain_b, bq_b, bk_b, bv_b, gain_two = vec_parts
     gain_full = gain_b.astype(jnp.float32)
     inv_rms = lax.rsqrt(jnp.mean(x_rows * x_rows, -1, keepdims=True) + norm_eps)
     normed = (x_rows * inv_rms * gain_full).astype(jnp.bfloat16)
@@ -263,11 +282,13 @@
     inv_rms_two = lax.rsqrt(jnp.mean(mid_rows * mid_rows, -1, keepdims=True) + norm_eps)
     normed_two = (mid_rows * inv_rms_two * gain_two_full).astype(jnp.bfloat16)
     cot_bf = cot_rows.astype(jnp.bfloat16)
-    normed_group, cot_group = (
-        lax.all_gather(normed_two, "wt", axis=0, tiled=True),
-        lax.all_gather(cot_bf, "wt", axis=0, tiled=True),
-    )
-    wg_own, wu_own, wd_own = unpack(row_bf[:, prefix:], n_wt, 9, 12)
+    pair_group = lax.all_gather(
+        jnp.concatenate([normed_two, cot_bf], 1), "wt", axis=0, tiled=True
+    )
+    normed_group = pair_group[:, :D]
+    cot_group = pair_group[:, D:]
+    ff_own = row_bf[0, prefix:].reshape(3 * (FF // n_wt), D)
+    wg_own, wu_own, wd_own = jnp.split(ff_own, 3, 0)
     gate_pre = inner_dot(normed_group, wg_own)
     up_pre = inner_dot(normed_group, wu_own)
     hidden_bf = hidden_units(gate_pre, up_pre)
@@ -403,12 +424,13 @@
         d_scaled * x_rows, -1, keepdims=True
     )
     input_grad = d_mid + d_input
-    mid_group, query_grads, key_grads_group, value_grads_group = (
-        lax.all_gather(d_mid_bf, "wt", axis=0, tiled=True),
-        lax.all_gather(dq_bf, "wt", axis=0, tiled=True),
-        lax.all_gather(dk_bf, "wt", axis=0, tiled=True),
-        lax.all_gather(dv_bf, "wt", axis=0, tiled=True),
-    )
+    back_group = lax.all_gather(
+        jnp.concatenate([d_mid_bf, dq_bf, dk_bf, dv_bf], 1), "wt", axis=0, tiled=True
+    )
+    mid_group = back_group[:, :D]
+    query_grads = back_group[:, D : D + QW]
+    key_grads_group = back_group[:, D + QW : D + QW + KEY_FEATURES]
+    value_grads_group = back_group[:, D + QW + KEY_FEATURES :]
     gain_part, gain_two_part = (
         lax.psum_scatter(grad_gain, "wt", scatter_dimension=0, tiled=True),
         lax.psum_scatter(grad_gain_two, "wt", scatter_dimension=0, tiled=True),
@@ -428,7 +450,16 @@
     bias_v = lax.dynamic_slice_in_dim(
         jnp.sum(value_grads_group.astype(jnp.float32), 0), wt_id * key_part_len, key_part_len, 0
     )
-    shard_grad = jnp.concatenate(
+    piece_len = moment1.shape[1]
+    piece_rows = -(-piece_len // D)
+    pad_rows = -(-piece_rows // 32) * 32
+    head_pieces = -(-prefix // piece_len)
+    ff_grad = jnp.concatenate(
+        [grad_wg, grad_wu, grad_wd, jnp.zeros((16, D), jnp.float32)], 0
+    )
+    spill = head_pieces * piece_len - prefix
+    spill_rows = -(-spill // D)
+    head = jnp.concatenate(
         [
             gain_part,
             grad_wq.reshape(-1),
@@ -439,13 +470,26 @@
             bias_v,
             grad_wo.reshape(-1),
             gain_two_part,
-            grad_wg.reshape(-1),
-            grad_wu.reshape(-1),
-            grad_wd.reshape(-1),
+            ff_grad[:spill_rows].reshape(-1)[:spill],
         ]
     )
-    grad_piece = lax.psum_scatter(shard_grad, "ctx", scatter_dimension=0, tiled=True)
-    piece_len = moment1.shape[1]
+    laid = []
+    for number in range(n_ctx):
+        start = number * piece_len
+        if number < head_pieces:
+            flat = jnp.pad(head[start : start + piece_len], (0, piece_rows * D - piece_len))
+            rows = flat.reshape(piece_rows, D)
+        else:
+            row_at, col_at = divmod(start - prefix, D)
+            rows = ff_grad[row_at : row_at + piece_rows]
+            if col_at:
+                after = ff_grad[row_at + 1 : row_at + 1 + piece_rows, :col_at]
+                rows = jnp.concatenate([rows[:, col_at:], after], 1)
+        laid.append(jnp.pad(rows.astype(jnp.bfloat16), ((0, pad_rows - piece_rows), (0, 0))))
+    own_rows = lax.psum_scatter(
+        jnp.concatenate(laid, 0), "ctx", scatter_dimension=0, tiled=True
+    )
+    grad_piece = own_rows.astype(jnp.float32).reshape(-1)[:piece_len]
     param_grad = grad_piece.reshape(1, piece_len)
     piece_start = ctx_id * piece_len
     own_params = lax.dynamic_slice_in_dim(params[0], piece_start, piece_len, 0).reshape(

time: 848 us -> 586 us (0.69)
  local copies, waits for them, and re-layouts: 272 us -> 146 us
  blocking collectives: 141 us -> 23.1 us
  waiting for transfers between devices: 268 us -> 247 us
  other arithmetic: 65.5 us -> 80.2 us
    unnamed x6 -> x7, waiting for transfers between devices: 195 us -> 0.11 us
    all_gather x6 -> x0, blocking collectives: 122 us -> none  [the longest x1 36.5 us: body(): lax.all_gather(cot_bf, 'wt', axis=0, tiled=True)]
    concatenate x1, local copies, waits for them, and re-layouts: 125 us -> 6.9 us  [body(): jnp.concatenate([gain_part, grad_wq.reshape(-1), bias_q, grad_wk.reshape(...]
    split x0 -> x4, local copies, waits for them, and re-layouts: none -> 74.4 us  [body(): wg_own, wu_own, wd_own = jnp.split(ff_own, 3, 0)]
    reduce_scatter x0 -> x1, waiting for transfers between devices: none -> 66.2 us  [body(): lax.psum_scatter(jnp.concatenate(laid, 0), 'ctx', scatter_dimension=0, ti...]
    slice x3, local copies, waits for them, and re-layouts: 52.9 us -> 9.3 us  [unpack(): piece = rows_arr[:, bounds[number] - base:bounds[number + 1] - base]]
    reduce_scatter x1, waiting for transfers between devices: 0.01 us -> 32.5 us  [body(): lax.psum_scatter(per_device, 'ctx', scatter_dimension=0, tiled=True)]
    reduce_scatter x1, waiting for transfers between devices: 0.01 us -> 31.1 us  [body(): lax.psum_scatter(jnp.dot(d_gate, wg_own, preferred_element_type=jnp.float...]
  transfers between devices with their start and end apart: 7 -> 9, of which waited for: 3 -> 7; matrix products, arithmetic and copies ran while one was open for 18% -> 20% of each run, Pallas kernels for 0% -> 0%
where the time goes in v1:
time: 586 us; the launch traced here: 576 us
  waiting for transfers between devices  247 us (42%)
  local copies, waits for them, and re-layouts  146 us (25%)
  other arithmetic  80.2 us (14%)
  matrix products  50.8 us (9%)
  blocking collectives  23.1 us (4%)
  between operations  19.1 us (3%)
  starting transfers between devices  8.27 us (1%)
    split x4, local copies, waits for them, and re-layouts, body(): wg_own, wu_own, wd_own = jnp.split(ff_own, 3, 0)  74.4 us
    all_gather x1, waiting for transfers between devices, body(): attn_all = lax.all_gather(attn_own, 'wt', axis=0, tiled=False)  74.1 us
    reduce_scatter x1, waiting for transfers between devices, body(): lax.psum_scatter(jnp.concatenate(laid, 0), 'ctx', scatter_dimension=0, ti...  66.2 us
    reduce_scatter x1, waiting for transfers between devices, body(): lax.psum_scatter(jnp.dot(hidden_bf, wd_own, preferred_element_type=jnp.fl...  39.6 us
    reduce_scatter x1, waiting for transfers between devices, body(): lax.psum_scatter(per_device, 'ctx', scatter_dimension=0, tiled=True)  32.5 us
    reduce_scatter x1, waiting for transfers between devices, body(): lax.psum_scatter(jnp.dot(d_gate, wg_own, preferred_element_type=jnp.float...  31.1 us
    sub x1, other arithmetic, body(): own_params - learn_rate * (m_hat / (jnp.sqrt(v_hat) + adam_eps) + decay_r...  31 us
    unnamed x1, blocking collectives  13.2 us
  transfers between devices with their start and end apart: 9, of which 7 were waited for; matrix products, arithmetic and copies ran while one was open for 20% of the time, Pallas kernels for 0%

profile of v1, /device:TPU:0, one launch (start us, length us, event | category | flops | bytes accessed | tf_op | source)
XLA Modules:
  0.0 575.6 jit_solution(7026509646285210157)
XLA Ops:
  7.2 12.8 %convert_element_type.170 = bf16[1,3728096]{1,0:T(2,128)(2,1)S(1)} convert(f32[1,3728096]{1,0:T(1,128)} %param.23) | non-fusion elementwise | flops 3728096 | bytes 22368576 | tf_op jit(solution)/shard_map/convert_element_type | solution.py:148
  20.9 4.4 copy-done
  25.3 8.5 %slice_reduce_fusion.4 = (bf16[200704]{0:T(1024)(128)(2,1)S(1)}, bf16[200704]{0:T(1024)(128)(2,1)S(1)}) fusion(bf16[1,3728096]{1,0:T(2,128)(2,1)S(1)} %convert_element_type.170), kind=kLoop, calls=%fused_computation.196 | loop fusion | bytes 1605632 | tf_op jit(solution)/shard_map/slice | solution.py:62
  41.1 74.1 %all-gather.9.cloned.1.call-done = bf16[960,2048]{1,0:T(8,128)(2,1)} async-done(((bf16[240,2048]{1,0:T(8,128)(2,1)}), bf16[960,2048]{1,0:T(8,128)(2,1)}) %all-gather.9.cloned.1.call-update) | async-done | bytes 3932176 | tf_op jit(solution)/shard_map/all_gather | solution.py:158
  115.2 4.4 slice.352
  121.1 1.2 fusion.106
  122.3 1.2 convolution_add_fusion.2
  123.6 9.9 %all_gather.17 = bf16[1024,256]{0,1:T(8,128)(2,1)S(1)} all-gather(bf16[128,256]{0,1:T(8,128)(2,1)S(1)} %pad_maximum_fusion.7), channel_id=1, replica_groups=mesh['ctx'=8,'wt'=4] {'ctx'}, dimensions={0}, use_global_device_ids=true | all-gather | bytes 589824 | tf_op jit(solution)/shard_map/all_gather | solution.py:190
  133.7 3.9 gather_fusion
  138.2 1.9 fusion.92
  140.7 1.2 while.74
  142.0 1.2 while.75
  144.0 2.4 while.76
  146.5 1.9 while.77
  149.3 2.0 multiply_reduce_fusion.2
  152.4 50.8 %slice_reduce_fusion = (bf16[1089536]{0:T(1024)(128)(2,1)}, bf16[1089536]{0:T(1024)(128)(2,1)}, bf16[1089536]{0:T(1024)(128)(2,1)}) fusion(bf16[1,3728096]{1,0:T(2,128)(2,1)} %copy-done), kind=kLoop, calls=%fused_computation.103 | loop fusion | bytes 13074432 | tf_op jit(solution)/shard_map/split | solution.py:291
  203.1 5.0 split.16
  208.1 5.0 split.18
  213.1 13.6 %split.20 = bf16[1216,896]{1,0:T(8,128)(2,1)} reshape(bf16[1089536]{0:T(1024)(128)(2,1)} %get-tuple-element.638) | data formatting | bytes 4358144 | tf_op jit(solution)/shard_map/split | solution.py:291
  226.8 3.5 fusion.135
  230.4 1.5 fusion.133
  232.0 3.5 multiply_convert_fusion
  235.5 1.5 fusion.202
  237.1 2.8 convolution_add_fusion
  239.9 4.8 fusion.201
  246.0 31.1 %reduce-scatter.7.cloned.1.call-done = f32[128,896]{1,0:T(8,128)} async-done(((f32[512,896]{1,0:T(8,128)}), f32[128,896]{1,0:T(8,128)}) %reduce-scatter.7.cloned.1.call-update) | async-done | bytes 458768 | tf_op jit(solution)/shard_map/reduce_scatter | solution.py:306
  277.2 1.8 multiply_reduce_fusion
  278.9 39.6 %reduce-scatter.5.cloned.1.call-done = f32[128,896]{1,0:T(8,128)} async-done(((f32[512,896]{1,0:T(8,128)}), f32[128,896]{1,0:T(8,128)}) %reduce-scatter.5.cloned.1.call-update) | async-done | bytes 458768 | tf_op jit(solution)/shard_map/reduce_scatter | solution.py:295
  318.5 2.3 fusion.191
  320.7 2.1 fusion.196
  323.6 2.6 while.78
  326.4 6.8 %while.79 = (s32[]{:T(128)}, f32[64,2,7,64]{0,3,2,1:T(8,128)S(1)}, f32[1024,256]{0,1:T(8,128)S(1)}, s32[]{:T(128)}, bf16[1024,256]{0,1:T(8,128)(2,1)S(1)}, /*ind...) while((s32[]{:T(128)}, f32[64,2,7,64]{0,3,2,1:T(8,128)S(1)}, ...), condition=%wide.region_25.26_spmd.clone, body=%wide.region_24.25_spmd.clone.sunk | while | flops 297747008 | bytes 12267235 | solution.py:381
  326.6 1.3 fusion.343
  329.8 1.3 fusion.343
  333.8 3.5 gather_fusion.1
  341.7 32.5 %reduce-scatter.9.cloned.1.call-done = f32[128,256]{0,1:T(8,128)} async-done(((f32[1024,256]{0,1:T(8,128)}), f32[128,256]{0,1:T(8,128)}) %reduce-scatter.9.cloned.1.call-update) | async-done | bytes 131088 | tf_op jit(solution)/shard_map/reduce_scatter | solution.py:410
  378.8 4.6 all-to-all-start
  385.4 2.7 fusion.131
  388.9 1.5 slice.385
  391.2 1.3 slice.387
  392.5 1.5 fusion.129
  396.0 1.5 fusion.125
  399.6 2.1 maximum_convert_fusion.1
  402.5 1.2 maximum_convert_fusion
  405.3 1.3 copy-done.3
  407.3 1.4 fusion.149
  408.7 13.2 %all-reduce.13 = (bf16[896]{0:T(1024)(128)(2,1)S(1)}, bf16[896]{0:T(1024)(128)(2,1)S(1)}) all-reduce(f32[896]{0:T(1024)S(1)} %get-tuple-element.652, f32[896]{0:T(1024)S(1)} %copy-done.45), channel_id=6, replica_groups=mesh['ctx'=8,'wt'=4] {'wt'}, use_global_device_ids=true, to_apply=%region_30.31.clone | all-reduce | flops 1792 | bytes 10752
  422.0 3.4 all-to-all-start.1
  426.3 1.7 convolution_convert_fusion.1
  429.7 2.2 all-to-all-done.1
  431.9 1.6 convolution_convert_fusion
  433.9 1.4 convert_reduce_fusion
  437.6 6.9 %concatenate.126 = bf16[466012]{0:T(1024)(128)(2,1)S(1)} concatenate(bf16[224]{0:T(256)(128)(2,1)S(1)} %dynamic-slice.24, bf16[200704]{0:T(1024)(128)(2,1)S(1)} %reshape.659, bf16[224]{0:T(256)(128)(2,1)S(1)} %dynamic_slice.54, bf16[28672]{0:T(1024)(128)(2,1)S(1)} %fusion.105, bf16[32]{0:T(256)(128)(2,1)S(1)} %dynamic_slice.56, bf16[28672]{0:T(1024)(128)(2,1)S(1)} %fusion.104, ...), dimensions={0} | concatenate | bytes 1864048 | tf_op jit(solution)/shard_map/concatenate | solution.py:462
  446.9 2.2 fusion.110
  449.1 1.2 fusion.112
  450.3 1.3 fusion.114
  451.6 1.3 fusion.116
  452.9 1.3 fusion.118
  454.3 1.4 fusion.120
  455.7 1.4 fusion.122
  459.2 66.2 %reduce-scatter.11.cloned.1.call-done = bf16[544,896]{1,0:T(8,128)(2,1)} async-done(((bf16[4352,896]{1,0:T(8,128)(2,1)}), bf16[544,896]{1,0:T(8,128)(2,1)}) %reduce-scatter.11.cloned.1.call-update) | async-done | bytes 974864 | tf_op jit(solution)/shard_map/reduce_scatter | solution.py:489
  525.4 2.0 reshape.664
  527.8 9.5 %reshape.665 = f32[1,466012]{1,0:T(1,128)} reshape(f32[466012]{0:T(1024)S(1)} %slice_convert_fusion) | data formatting | bytes 3728096 | tf_op jit(solution)/shard_map/reshape | solution.py:493
  537.3 31.0 %multiply_subtract_fusion = (f32[1,466012]{1,0:T(1,128)}, f32[1,466012]{1,0:T(1,128)}, f32[1,466012]{1,0:T(1,128)}) fusion(f32[1,3728096]{1,0:T(1,128)} %param.23, s32[]{:T(128)S(6)} %select_n.312, s32[]{:T(128)S(6)} %mul.563, f32[466012]{0:T(1024)S(1)} %get-tuple-element.779, f32[1,466012]{1,0:T(1,128)S(1)} %copy-done.24, ...), kind=kLoop, calls=%fused_computation.139 | loop fusion | flops 22368576 | bytes 14912392 | tf_op jit(solution)/shard_map/sub | solution.py:505
  (350 shorter events, 55.3 us)
Async XLA Ops:
  7.2 108.0 %all-gather.9.cloned.1.call-start = ((), (), s32[]{:S(2)}) async-start(), calls=%async_computation.12 | async-start | bytes 4915200 | tf_op jit(solution)/shard_map/all_gather | solution.py:158
  20.0 5.3 copy-start
  34.4 1.6 copy-start.53
  34.4 5.0 copy-start.57
  34.4 5.3 copy-start.6
  34.8 5.5 copy-start.26
  35.9 190.9 %all-gather.5.cloned.1.call-start = ((), (), s32[]{:S(2)}) async-start(), calls=%async_computation.6 | async-start | bytes 2293760 | tf_op jit(solution)/shard_map/all_gather | solution.py:285
  39.5 100.7 %copy-start.38 = (f32[128,64]{0,1:T(8,128)}, f32[128,64]{0,1:T(8,128)S(1)}, u32[]{:S(2)}) copy-start(f32[128,64]{0,1:T(8,128)S(1)} %get-tuple-element.812) | copy-start | bytes 98308
  39.6 100.7 %copy-start.40 = (f32[128,64]{0,1:T(8,128)}, f32[128,64]{0,1:T(8,128)S(1)}, u32[]{:S(2)}) copy-start(f32[128,64]{0,1:T(8,128)S(1)} %get-tuple-element.813) | copy-start | bytes 98308
  40.3 80.7 %copy-start.50 = (f32[128]{0:T(128)}, f32[128]{0:T(128)S(1)}, u32[]{:S(2)}) copy-start(f32[128]{0:T(128)S(1)} %get-tuple-element.805) | copy-start | bytes 1540
  148.5 2.8 copy-start.49
  149.2 2.2 copy-start.37
  152.3 124.9 %reduce-scatter.7.cloned.1.call-start = ((), (), s32[]{:S(2)}) async-start(), calls=%async_computation.8 | async-start | bytes 2293760 | tf_op jit(solution)/shard_map/reduce_scatter | solution.py:306
  226.8 3.6 copy-start.19
  226.8 3.6 copy-start.55
  230.4 1.6 copy-start.8
  232.0 3.5 copy-start.9
  235.5 1.5 copy-start.34
  235.5 1.6 copy-start.59
  239.9 78.6 %reduce-scatter.5.cloned.1.call-start = ((), (), s32[]{:S(2)}) async-start(), calls=%async_computation.7 | async-start | bytes 2293760 | tf_op jit(solution)/shard_map/reduce_scatter | solution.py:295
  244.7 73.8 %copy-start.27 = (f32[1,128,896]{2,1,0:T(8,128)S(1)}, f32[1,128,896]{2,1,0:T(8,128)}, u32[]{:S(2)}) copy-start(f32[1,128,896]{2,1,0:T(8,128)} %param.20) | copy-start | bytes 1376260
  244.7 129.5 %reduce-scatter.9.cloned.1.call-start = ((), (), s32[]{:S(2)}) async-start(), calls=%async_computation.9 | async-start | bytes 1179648 | tf_op jit(solution)/shard_map/reduce_scatter | solution.py:410
  320.7 2.1 copy-start.22
  338.0 1.1 copy-start.7
  338.0 1.4 copy-start.39
  339.0 87.3 %all-gather.7.cloned.1.call-start = ((), (), s32[]{:S(2)}) async-start(), calls=%async_computation.10 | async-start | bytes 2621440 | tf_op jit(solution)/shard_map/all_gather | solution.py:427
  339.1 1.9 copy-start.41
  341.4 35.7 %copy-start.23 = (bf16[128,896]{1,0:T(8,128)(2,1)S(1)}, bf16[128,896]{1,0:T(8,128)(2,1)}, u32[]{:S(2)}) copy-start(bf16[128,896]{1,0:T(8,128)(2,1)} %copy-done.22) | copy-start | bytes 688132
  341.6 36.4 %copy-start.51 = (f32[128]{0:T(128)S(1)}, f32[128]{0:T(128)}, u32[]{:S(2)}) copy-start(f32[128]{0:T(128)} %copy-done.50) | copy-start | bytes 1540
  341.7 41.8 %copy-start.13 = (f32[2,7,64,64]{3,2,1,0:T(8,128)S(1)}, f32[2,7,64,64]{3,2,1,0:T(8,128)}, u32[]{:S(2)}) copy-start(f32[2,7,64,64]{3,2,1,0:T(8,128)} %copy-done.12) | copy-start | bytes 688132
  377.9 6.0 %copy-start.11 = (f32[2,7,64,64]{3,2,1,0:T(8,128)S(1)}, f32[2,7,64,64]{3,2,1,0:T(8,128)}, u32[]{:S(2)}) copy-start(f32[2,7,64,64]{3,2,1,0:T(8,128)} %copy-done.10) | copy-start | bytes 688132
  378.8 43.2 %all-to-all-start = ((bf16[128,4,224]{0,2,1:T(8,128)(2,1)}), bf16[128,4,224]{0,2,1:T(8,128)(2,1)S(1)}, u32[]{:S(2)}, u32[]{:S(2)}) async-start(bf16[128,4,224]{0,2,1:T(8,128)(2,1)} %multiply_convert_fusion.3), calls=%async_computation.3 | async-start | bytes 458752 | tf_op jit(solution)/shard_map/all_to_all | solution.py:277
  383.5 2.0 copy-start.35
  388.1 4.4 copy-start.4
  388.9 3.6 copy-start.56
  388.9 3.6 copy-start.60
  394.0 2.0 copy-start.33
  397.4 1.9 copy-start.1
  397.5 2.1 slice-start
  399.6 2.1 copy-start.5
  402.5 1.8 copy-start.2
  404.4 2.3 copy-start.3
  405.3 1.5 copy-start.42
  407.3 1.4 copy-start.45
  422.0 3.4 copy-start.43
  422.0 9.9 %all-to-all-start.1 = ((bf16[128,4,224]{0,2,1:T(8,128)(2,1)}), bf16[128,4,224]{0,2,1:T(8,128)(2,1)S(1)}, u32[]{:S(2)}, u32[]{:S(2)}) async-start(bf16[128,4,224]{0,2,1:T(8,128)(2,1)} %copy.174), calls=%async_computation.4 | async-start | bytes 458752 | tf_op jit(solution)/shard_map/all_to_all | solution.py:278
  425.4 99.9 %reduce-scatter.11.cloned.1.call-start = ((), (), s32[]{:S(2)}) async-start(), calls=%async_computation.11 | async-start | bytes 8773632 | tf_op jit(solution)/shard_map/reduce_scatter | solution.py:489
  428.4 6.9 %copy-start.44 = (bf16[128,4,224]{0,2,1:T(8,128)(2,1)S(1)}, bf16[128,4,224]{0,2,1:T(8,128)(2,1)}, u32[]{:S(2)}) copy-start(bf16[128,4,224]{0,2,1:T(8,128)(2,1)} %copy-done.43) | copy-start | bytes 688132
  445.5 1.4 copy-start.15
  445.5 3.6 copy-start.18
  445.5 3.6 copy-start.31
  446.9 3.4 copy-start.20
  446.9 3.4 copy-start.21
  449.1 2.5 copy-start.17
  449.1 2.5 copy-start.30
  450.3 2.6 copy-start.16
  450.3 2.6 copy-start.32
  451.6 2.7 copy-start.14
  451.6 2.7 copy-start.36
  457.1 1.0 copy-start.28
  457.1 1.2 copy-start.29
  457.1 1.2 copy-start.54
  527.8 9.5 %copy-start.24 = (f32[1,466012]{1,0:T(1,128)S(1)}, f32[1,466012]{1,0:T(1,128)}, u32[]{:S(2)}) copy-start(f32[1,466012]{1,0:T(1,128)} %param.24) | copy-start | bytes 5592148
  527.8 9.5 %copy-start.25 = (f32[1,466012]{1,0:T(1,128)S(1)}, f32[1,466012]{1,0:T(1,128)}, u32[]{:S(2)}) copy-start(f32[1,466012]{1,0:T(1,128)} %param.25) | copy-start | bytes 5592148
  (7 other events, 5.0 us)
Sparse Core Ops, SparseCore 0:
  36.0 79.1 all-gather.8
  152.4 38.9 all-gather.4
  240.0 37.1 reduce-scatter.6
  279.9 38.5 reduce-scatter.4
  339.2 35.0 reduce-scatter.8
  378.1 48.1 all-gather.6
  457.3 68.0 reduce-scatter.10
